TPU v7x, 32 devices: a whole 2x2x4 slice. The times are simulated.
32 devices in a mesh: fsdp: 8 (over y, x, core), tp: 4 (over z).
Axes of the slice: x: 2, y: 2, z: 4, core: 2. Of those that a mesh axis runs over, the one named last changes fastest.
Arguments:
- residual: bfloat16 [4096, 2048], P(('fsdp', 'tp')), may hold values from -6 to 6
- norm_gain: bfloat16 [2048], P(('fsdp', 'tp')), may hold values from 0.099609375 to 1.8984375
- norm_shift: bfloat16 [2048], P(('fsdp', 'tp')), may hold values from -1.75 to 1.75
- qkv_weight: bfloat16 [3, 2048, 2048], P(None, 'fsdp', 'tp'), may hold values from -0.125 to 0.125
- qkv_bias: bfloat16 [3, 2048], P(None, ('tp', 'fsdp')), may hold values from -1.75 to 1.75
- dense_weight: bfloat16 [2048, 2048], P('tp', 'fsdp'), may hold values from -0.75 to 0.75
- dense_bias: bfloat16 [2048], P(('fsdp', 'tp')), may hold values from -1.75 to 1.75
- inner_weight: bfloat16 [2048, 8192], P('fsdp', 'tp'), may hold values from -0.125 to 0.125
- inner_bias: bfloat16 [8192], P(('tp', 'fsdp')), may hold values from -1.75 to 1.75
- outer_weight: bfloat16 [8192, 2048], P('tp', 'fsdp'), may hold values from -0.0625 to 0.0625
- outer_bias: bfloat16 [2048], P(('fsdp', 'tp')), may hold values from -1.75 to 1.75
- cotangent: bfloat16 [4096, 2048], P(('fsdp', 'tp')), may hold values from -6 to 6
- segment: int32 [4096], replicated, may hold values from 0 to 38, as said below
- ancestors: int32 [39, 3], replicated, may hold values from 0 to 38, as said below
- valid_slot: int32 [4096], replicated, may hold values from 0 to 1, as said below
Outputs:
- output: bfloat16 [4096, 2048], P(('fsdp', 'tp'))
- residual_grad: bfloat16 [4096, 2048], P(('fsdp', 'tp'))
- norm_gain_grad: float32 [2048], P(('fsdp', 'tp'))
- norm_shift_grad: float32 [2048], P(('fsdp', 'tp'))
- qkv_weight_grad: float32 [3, 2048, 2048], P(None, 'fsdp', 'tp')
- qkv_bias_grad: float32 [3, 2048], P(None, ('tp', 'fsdp'))
- dense_weight_grad: float32 [2048, 2048], P('tp', 'fsdp')
- dense_bias_grad: float32 [2048], P(('fsdp', 'tp'))
- inner_weight_grad: float32 [2048, 8192], P('fsdp', 'tp')
- inner_bias_grad: float32 [8192], P(('tp', 'fsdp'))
- outer_weight_grad: float32 [8192, 2048], P('tp', 'fsdp')
- outer_bias_grad: float32 [2048], P(('fsdp', 'tp'))
Inputs may be any that keep to these rules, and one draw needn't show every extreme that they name: Each of the 3 trees fills 1024 consecutive slots, in order of slots: a trunk of 640 slots, then four branches and eight leaves of 32 slots each, two leaves to a branch, each leaf after its branch; the slots of a segment are consecutive and carry its id; padding slots carry 0. `ancestors`: row s names the trunk, branch and leaf segment of the path that ends in segment s, repeating s where the path is shorter; each tree's segments name only that tree's segments. `valid_slot`: 1 on exactly the slots that trees fill, 0 on the other 1024 slots.
All inputs are finite; a program needn't handle non-finite values.
Results may differ from a plain program's by a relative error of at most 0.0098.
Values may be sent and summed in bfloat16 or wider, within the bound.
No kernel may reach another device: no remote copies, remote signals or barrier semaphores. Data moves between devices by JAX's collectives and lax.ppermute only.
A program may use at most 192 MiB of HBM per device.

v0:
```python
import jax
import jax.numpy as jnp
from jax import lax
from jax.sharding import PartitionSpec as P

HEAD_DIM = 64
ROTARY = 32
TREE_LEN = 1024
EPSILON = 1e-05


def passed_along(value, axis, steps):
    count = lax.axis_size(axis)
    initial, last = (max(0, -steps), min(count, count - steps))
    return lax.ppermute(value, axis, [(source, source + steps) for source in range(initial, last)])


def norm_rows(inputs_f, gain_f, shift_f):
    row_mean = jnp.mean(inputs_f, axis=-1, keepdims=True)
    centered = inputs_f - row_mean
    variance = jnp.mean(centered * centered, axis=-1, keepdims=True)
    return centered * lax.rsqrt(variance + EPSILON) * gain_f + shift_f


def tree_allowed(query_seg, query_slot, query_valid, key_seg, key_slot, key_valid, ancestors):
    seg_ids = jnp.arange(ancestors.shape[0], dtype=jnp.int32)
    onehot = (query_seg[:, None] == seg_ids[None, :]).astype(jnp.int32)
    path_ids = jnp.sum(onehot[:, :, None] * ancestors[None, :, :], axis=1)
    linked = (
        (key_seg[None, :] == path_ids[:, 0:1])
        | (key_seg[None, :] == path_ids[:, 1:2])
        | (key_seg[None, :] == path_ids[:, 2:3])
    )
    earlier = key_slot[None, :] <= query_slot[:, None]
    usable = (key_valid[None, :] == 1) & (query_valid[:, None] == 1)
    return linked & earlier & usable | (key_slot[None, :] == query_slot[:, None])


def rotate(tensor, positions, direction):
    half_rot = ROTARY // 2
    freq = 10000.0 ** (-(jnp.arange(half_rot, dtype=jnp.float32) * 2.0 / ROTARY))
    angle = direction * positions.astype(jnp.float32)[:, None] * freq[None, :]
    cosine = jnp.cos(angle)[:, None, :]
    sine = jnp.sin(angle)[:, None, :]
    first = tensor[..., :half_rot]
    second = tensor[..., half_rot:ROTARY]
    return jnp.concatenate(
        [first * cosine - second * sine, second * cosine + first * sine, tensor[..., ROTARY:]],
        axis=-1,
    )


def body(
    residual,
    norm_gain,
    norm_shift,
    qkv_weight,
    qkv_bias,
    dense_weight,
    dense_bias,
    inner_weight,
    inner_bias,
    outer_weight,
    outer_bias,
    cotangent,
    segment,
    ancestors,
    valid_slot,
):
    f32 = jnp.float32
    bf16 = jnp.bfloat16
    tp_size = lax.axis_size("tp")
    local_rows = residual.shape[0]
    group_rows = local_rows * tp_size
    head_cols = qkv_weight.shape[2]
    head_count = head_cols // HEAD_DIM
    reach_back = (TREE_LEN - 2) // group_rows + 1
    front_rows = reach_back * group_rows
    window = front_rows + group_rows
    block_rows = min(512, group_rows)
    block_count = group_rows // block_rows
    scaling = HEAD_DIM ** (-0.5)
    base_slot = lax.axis_index("fsdp") * group_rows
    vectors = (
        lax.all_gather(norm_gain, ("fsdp", "tp"), axis=0, tiled=True),
        lax.all_gather(norm_shift, ("fsdp", "tp"), axis=0, tiled=True),
        lax.all_gather(dense_bias, ("fsdp", "tp"), axis=0, tiled=True),
        lax.all_gather(outer_bias, ("fsdp", "tp"), axis=0, tiled=True),
    )
    gain_f = vectors[0].astype(f32)
    shift_f = vectors[1].astype(f32)
    bias_sum = vectors[2].astype(f32) + vectors[3].astype(f32)
    seg_front = jnp.concatenate([jnp.zeros((front_rows,), jnp.int32), segment])
    valid_front = jnp.concatenate([jnp.zeros((front_rows,), jnp.int32), valid_slot])
    query_slot = base_slot + jnp.arange(group_rows, dtype=jnp.int32)
    query_seg = lax.dynamic_slice_in_dim(segment, base_slot, group_rows)
    query_valid = lax.dynamic_slice_in_dim(valid_slot, base_slot, group_rows)
    key_slot = base_slot - front_rows + jnp.arange(window, dtype=jnp.int32)
    key_seg = lax.dynamic_slice_in_dim(seg_front, base_slot, window)
    key_valid = lax.dynamic_slice_in_dim(valid_front, base_slot, window)

    def allowed_for():
        return tree_allowed(
            query_seg, query_slot, query_valid, key_seg, key_slot, key_valid, ancestors
        )

    def count_keys(block_num):
        return jnp.sum(allowed_for().astype(jnp.int32), axis=1) - 1

    block_ids = jnp.arange(block_count, dtype=jnp.int32)
    positions = lax.map(count_keys, block_ids).reshape(group_rows)
    inputs_f = residual.astype(f32)
    normed_local = norm_rows(inputs_f, gain_f, shift_f).astype(bf16)

    def key_window(keys_own, values_own):
        key_parts = []
        value_parts = []
        for distance in range(reach_back, 0, -1):
            got_keys, got_values = passed_along((keys_own, values_own), "fsdp", distance)
            key_parts.append(got_keys)
            value_parts.append(got_values)
        return (
            jnp.concatenate(key_parts + [keys_own], axis=0),
            jnp.concatenate(value_parts + [values_own], axis=0),
        )

    def forward_pieces():
        gathered = (
            lax.all_gather(qkv_weight, "fsdp", axis=1, tiled=True),
            lax.all_gather(qkv_bias, "fsdp", axis=1, tiled=True),
            lax.all_gather(dense_weight, "fsdp", axis=1, tiled=True),
            lax.all_gather(inner_weight, "fsdp", axis=0, tiled=True),
            lax.all_gather(inner_bias, "fsdp", axis=0, tiled=True),
            lax.all_gather(outer_weight, "fsdp", axis=1, tiled=True),
        )
        normed = lax.all_gather(normed_local, "tp", axis=0, tiled=True)
        w_qkv = gathered[0]
        mixed = (
            jnp.einsum("td,sde->ste", normed, w_qkv, preferred_element_type=f32)
            + gathered[1].astype(f32)[:, None, :]
        )
        queries = rotate(mixed[0].reshape(group_rows, head_count, HEAD_DIM), positions, 1.0).astype(
            bf16
        )
        keys_own = (
            rotate(mixed[1].reshape(group_rows, head_count, HEAD_DIM), positions, 1.0)
            .astype(bf16)
            .reshape(group_rows, head_cols)
        )
        values_own = mixed[2].astype(bf16)
        keys_win, values_win = key_window(keys_own, values_own)
        keys_win = keys_win.reshape(window, head_count, HEAD_DIM)
        values_win = values_win.reshape(window, head_count, HEAD_DIM)

        def attend(block_num):
            scores = (
                jnp.einsum("qhe,khe->hqk", queries, keys_win, preferred_element_type=f32) * scaling
            )
            scores = jnp.where(allowed_for()[None], scores, -jnp.inf)
            top_score = jnp.max(scores, axis=-1, keepdims=True)
            expo = jnp.exp(scores - top_score)
            summed = jnp.sum(expo, axis=-1, keepdims=True)
            probs_low = (expo / summed).astype(bf16)
            attended = jnp.einsum("hqk,khe->qhe", probs_low, values_win, preferred_element_type=f32)
            return (attended, (top_score + jnp.log(summed))[..., 0])

        attended, log_sums = lax.map(attend, block_ids)
        attended = attended.reshape(group_rows, head_cols).astype(bf16)
        pre_act = jnp.dot(normed, gathered[3], preferred_element_type=f32) + gathered[4].astype(f32)
        activated = jax.nn.gelu(pre_act, approximate=True).astype(bf16)
        return (
            gathered,
            normed,
            queries,
            keys_win,
            values_win,
            attended,
            log_sums,
            pre_act,
            activated,
        )

    gathered, normed, queries, keys_win, values_win, attended, log_sums, pre_act, activated = (
        forward_pieces()
    )
    partial_rows = jnp.dot(attended, gathered[2], preferred_element_type=f32) + jnp.dot(
        activated, gathered[5], preferred_element_type=f32
    )
    summed_rows = lax.psum_scatter(partial_rows, "tp", scatter_dimension=0, tiled=True)
    output = (inputs_f + summed_rows + bias_sum).astype(bf16)
    out_bias_grad = jnp.sum(cotangent.astype(f32), axis=0)
    grad_rows = lax.all_gather(cotangent, "tp", axis=0, tiled=True)
    gathered, normed, queries, keys_win, values_win, attended, log_sums, pre_act, activated = (
        forward_pieces()
    )
    w_qkv = gathered[0]
    w_dense = gathered[2]
    w_inner = gathered[3]
    w_outer = gathered[5]
    outer_grad = jnp.einsum("tf,td->fd", activated, grad_rows, preferred_element_type=f32)
    act_grad = jnp.einsum("td,fd->tf", grad_rows, w_outer, preferred_element_type=f32)
    unused_value, gelu_pull = jax.vjp(
        lambda inputs_g: jax.nn.gelu(inputs_g, approximate=True), pre_act
    )
    pre_grad = gelu_pull(act_grad)[0].astype(bf16)
    inner_grad = jnp.einsum("td,tf->df", normed, pre_grad, preferred_element_type=f32)
    inner_bias_grad = jnp.sum(pre_grad.astype(f32), axis=0)
    normed_grad = jnp.einsum("tf,df->td", pre_grad, w_inner, preferred_element_type=f32)
    dense_grad = jnp.einsum("tc,td->cd", attended, grad_rows, preferred_element_type=f32)
    attn_grad = (
        jnp.einsum("td,cd->tc", grad_rows, w_dense, preferred_element_type=f32)
        .astype(bf16)
        .reshape(group_rows, head_count, HEAD_DIM)
    )

    def attend_back(carry, inputs_b):
        key_acc, value_acc = carry
        block_num, log_block = inputs_b
        scores = jnp.einsum("qhe,khe->hqk", queries, keys_win, preferred_element_type=f32) * scaling
        probs = jnp.where(allowed_for()[None], jnp.exp(scores - log_block[..., None]), 0.0)
        probs_low = probs.astype(bf16)
        prob_grad = jnp.einsum("qhe,khe->hqk", attn_grad, values_win, preferred_element_type=f32)
        row_dot = jnp.sum(probs * prob_grad, axis=-1, keepdims=True)
        score_grad = (probs * (prob_grad - row_dot)).astype(bf16)
        query_grad = (
            jnp.einsum("hqk,khe->qhe", score_grad, keys_win, preferred_element_type=f32) * scaling
        )
        key_part = (
            key_acc
            + jnp.einsum("hqk,qhe->khe", score_grad, queries, preferred_element_type=f32) * scaling
        )
        value_part = value_acc + jnp.einsum(
            "hqk,qhe->khe", probs_low, attn_grad, preferred_element_type=f32
        )
        key_acc = key_part
        value_acc = value_part
        return ((key_acc, value_acc), query_grad)

    zero_window = jnp.zeros((window, head_count, HEAD_DIM), f32)
    (key_acc, value_acc), query_grads = lax.scan(
        attend_back, (zero_window, zero_window), (block_ids, log_sums)
    )
    key_flat = key_acc.reshape(window, head_cols)
    value_flat = value_acc.reshape(window, head_cols)
    own_key = key_flat[front_rows:]
    own_value = value_flat[front_rows:]
    for distance in range(1, reach_back + 1):
        lower = front_rows - distance * group_rows
        got_key, got_value = passed_along(
            (key_flat[lower : lower + group_rows], value_flat[lower : lower + group_rows]),
            "fsdp",
            -distance,
        )
        own_key = own_key + got_key
        own_value = own_value + got_value
    query_pre = rotate(
        query_grads.reshape(group_rows, head_count, HEAD_DIM), positions, -1.0
    ).reshape(group_rows, head_cols)
    key_pre = rotate(own_key.reshape(group_rows, head_count, HEAD_DIM), positions, -1.0).reshape(
        group_rows, head_cols
    )
    qkv_grad = jnp.stack([query_pre, key_pre, own_value]).astype(bf16)
    qkv_weight_part = jnp.einsum("td,ste->sde", normed, qkv_grad, preferred_element_type=f32)
    qkv_bias_part = jnp.sum(qkv_grad.astype(f32), axis=1)
    normed_grad = normed_grad + jnp.einsum(
        "ste,sde->td", qkv_grad, w_qkv, preferred_element_type=f32
    )
    local_grad = lax.psum_scatter(normed_grad, "tp", scatter_dimension=0, tiled=True)
    unused_norm, norm_pull = jax.vjp(norm_rows, inputs_f, gain_f, shift_f)
    input_grad, gain_grad, shift_grad = norm_pull(local_grad)
    residual_grad = (cotangent.astype(f32) + input_grad).astype(bf16)
    weight_sums = (
        lax.psum_scatter(qkv_weight_part, "fsdp", scatter_dimension=1, tiled=True),
        lax.psum_scatter(qkv_bias_part, "fsdp", scatter_dimension=1, tiled=True),
        lax.psum_scatter(dense_grad, "fsdp", scatter_dimension=1, tiled=True),
        lax.psum_scatter(inner_grad, "fsdp", scatter_dimension=0, tiled=True),
        lax.psum_scatter(inner_bias_grad, "fsdp", scatter_dimension=0, tiled=True),
        lax.psum_scatter(outer_grad, "fsdp", scatter_dimension=1, tiled=True),
    )
    vector_sums = (
        lax.psum_scatter(gain_grad, ("fsdp", "tp"), scatter_dimension=0, tiled=True),
        lax.psum_scatter(shift_grad, ("fsdp", "tp"), scatter_dimension=0, tiled=True),
        lax.psum_scatter(out_bias_grad, ("fsdp", "tp"), scatter_dimension=0, tiled=True),
    )
    return (
        output,
        residual_grad,
        vector_sums[0],
        vector_sums[1],
        weight_sums[0],
        weight_sums[1],
        weight_sums[2],
        vector_sums[2],
        weight_sums[3],
        weight_sums[4],
        weight_sums[5],
        vector_sums[2],
    )


def solution(mesh):
    return jax.shard_map(
        body,
        mesh=mesh,
        in_specs=(
            P(("fsdp", "tp"), None),
            P(("fsdp", "tp")),
            P(("fsdp", "tp")),
            P(None, "fsdp", "tp"),
            P(None, ("tp", "fsdp")),
            P("tp", "fsdp"),
            P(("fsdp", "tp")),
            P("fsdp", "tp"),
            P(("tp", "fsdp")),
            P("tp", "fsdp"),
            P(("fsdp", "tp")),
            P(("fsdp", "tp"), None),
            P(),
            P(),
            P(),
        ),
        out_specs=(
            P(("fsdp", "tp"), None),
            P(("fsdp", "tp"), None),
            P(("fsdp", "tp")),
            P(("fsdp", "tp")),
            P(None, "fsdp", "tp"),
            P(None, ("tp", "fsdp")),
            P("tp", "fsdp"),
            P(("fsdp", "tp")),
            P("fsdp", "tp"),
            P(("tp", "fsdp")),
            P("tp", "fsdp"),
            P(("fsdp", "tp")),
        ),
        check_vma=False,
    )
```

profile of v0, /device:TPU:0, one launch (start us, length us, event | category | flops | bytes accessed | tf_op | source)
XLA Modules:
  0.0 1016.9 jit_solution(10757736382496534110)
XLA Ops:
  10.7 42.2 %all-reduce.11 = (bf16[2048]{0:T(1024)(128)(2,1)S(1)}, bf16[2048]{0:T(1024)(128)(2,1)S(1)}, bf16[2048]{0:T(1024)(128)(2,1)}, bf16[2048]{0:T(1024)(128)(2,1)}) all-reduce(bf16[2048]{0:T(1024)(128)(2,1)S(1)} %dynamic-update-slice.1, bf16[2048]{0:T(1024)(128)(2,1)S(1)} %dynamic-update-slice, ...), channel_id=1, replica_groups=mesh['fsdp'=8,'tp'=4] {'fsdp','tp'}, use_global_device_ids=true, to_apply=%add.3 | all-reduce | flops 8192 | bytes 32768
  65.6 10.2 %all-gather = bf16[8,64,3]{1,2,0:T(4,128)(2,1)S(1)} all-gather(bf16[1,64,3]{1,2,0:T(4,128)(2,1)S(1)} %bitcast.110), channel_id=1, replica_groups=mesh['fsdp'=8,'tp'=4] {'fsdp'}, dimensions={0}, use_global_device_ids=true | all-gather | bytes 3456 | tf_op jit(solution)/shard_map/all_gather | solution.py:130
  75.9 7.9 all-gather.1
  85.4 19.4 %all-gather.9.cloned.1.call-done = bf16[512,2048]{1,0:T(8,128)(2,1)} async-done(((bf16[128,2048]{1,0:T(8,128)(2,1)}), bf16[512,2048]{1,0:T(8,128)(2,1)}) %all-gather.9.cloned.1.call-update) | async-done | bytes 2097168 | tf_op jit(solution)/shard_map/all_gather | solution.py:136
  104.8 47.9 %all-gather.11.cloned.1.call-done = bf16[3,2048,512]{1,2,0:T(8,128)(2,1)} async-done(((bf16[3,256,512]{1,2,0:T(8,128)(2,1)}), bf16[3,2048,512]{1,2,0:T(8,128)(2,1)}) %all-gather.11.cloned.1.call-update) | async-done | bytes 6291472 | tf_op jit(solution)/shard_map/all_gather | solution.py:129
  167.4 32.8 %all-gather.19.cloned.1.call-done = bf16[512,2048]{1,0:T(8,128)(2,1)} async-done(((bf16[128,2048]{1,0:T(8,128)(2,1)}), bf16[512,2048]{1,0:T(8,128)(2,1)}) %all-gather.19.cloned.1.call-update) | async-done | bytes 2097168 | tf_op jit(solution)/shard_map/all_gather | solution.py:192
  200.2 28.7 %all-gather.13.cloned.1.call-done = bf16[512,2048]{1,0:T(8,128)(2,1)} async-done(((bf16[512,256]{1,0:T(8,128)(2,1)}), bf16[512,2048]{1,0:T(8,128)(2,1)}) %all-gather.13.cloned.1.call-update) | async-done | bytes 2097168 | tf_op jit(solution)/shard_map/all_gather | solution.py:131
  239.4 11.9 %select_reduce_fusion = (f32[8,512]{1,0:T(8,128)S(1)}, f32[8,512,1536]{2,1,0:T(8,128)}) fusion(pred[512,1536]{1,0:T(8,128)(4,1)S(1)} %get-tuple-element.236, bf16[512,8,64]{0,2,1:T(8,128)(2,1)S(1)} %maximum_convert_fusion, bf16[512,8,64]{0,2,1:T(8,128)(2,1)} %bitcast.14, bf16[512,8,64]{0,2,1:T(8,128)(2,1)} %bitcast.13, bf16[512,8,32]{0,2,1:T(8,128)(2,1)S(1)} %slice.202, ...), kind=kOutput, calls=%fused_computation.5 | convolution fusion | flops 830468096 | bytes 28065792 | tf_op jit(solution)/shard_map/while/body/eval_jaxpr/qhe,khe->hqk/dot_general | solution.py:157
  251.3 11.6 %fusion = f32[8,512]{1,0:T(8,128)S(1)} fusion(f32[8,512,1536]{2,1,0:T(8,128)} %get-tuple-element.268, f32[8,512]{1,0:T(8,128)S(1)} %get-tuple-element.267, pred[512,1536]{1,0:T(8,128)(4,1)S(1)} %get-tuple-element.236), kind=kLoop, calls=%fused_computation.6 | loop fusion | flops 25161728 | bytes 25985024 | tf_op jit(solution)/shard_map/while/body/eval_jaxpr/reduce_sum | solution.py:162
  263.5 19.6 %multiply_reduce_fusion = (f32[8,512]{1,0:T(8,128)S(1)}, f32[8,512,1536]{2,1,0:T(8,128)}) fusion(f32[8,512,1536]{2,1,0:T(8,128)} %get-tuple-element.268, f32[8,512]{1,0:T(8,128)S(1)} %log_add_fusion, pred[512,1536]{1,0:T(8,128)(4,1)S(1)} %get-tuple-element.236, bf16[512,8,64]{0,2,1:T(8,128)(2,1)S(1)} %bitcast.100, bf16[1536,8,64]{0,2,1:T(8,128)(2,1)S(1)} %bitcast.82), kind=kOutput, calls=%fused_computation.1 | convolution fusion | flops 836759552 | bytes 53248000 | tf_op jit(solution)/shard_map/while/body/eval_jaxpr/qhe,khe->hqk/dot_general | solution.py:222
  283.1 17.4 %multiply_convert_fusion = bf16[8,512,1536]{2,1,0:T(8,128)(2,1)S(1)} fusion(f32[8,512,1536]{2,1,0:T(8,128)} %get-tuple-element.270, f32[8,512,1536]{2,1,0:T(8,128)} %get-tuple-element.268, f32[8,512]{1,0:T(8,128)S(1)} %get-tuple-element.269, f32[8,512]{1,0:T(8,128)S(1)} %log_add_fusion, pred[512,1536]{1,0:T(8,128)(4,1)S(1)} %get-tuple-element.236), kind=kLoop, calls=%fused_computation | loop fusion | flops 37748736 | bytes 63733760 | tf_op jit(solution)/shard_map/while/body/eval_jaxpr/convert_element_type | solution.py:224
  309.8 10.9 %fusion.14 = f32[1536,8,64]{0,2,1:T(8,128)S(1)} fusion(bf16[512,8,64]{0,2,1:T(8,128)(2,1)S(1)} %bitcast.101, f32[8,512,1536]{2,1,0:T(8,128)} %get-tuple-element.268, f32[8,512]{1,0:T(8,128)S(1)} %log_add_fusion, pred[512,1536]{1,0:T(8,128)(4,1)S(1)} %get-tuple-element.236), kind=kOutput, calls=%fused_computation.26 | convolution fusion | flops 830472192 | bytes 29638656 | tf_op jit(solution)/shard_map/while/body/eval_jaxpr/hqk,qhe->khe/dot_general | solution.py:232
  328.8 9.0 fusion.26
  340.4 22.6 %collective-permute-done.5 = f32[512,512]{0,1:T(8,128)} collective-permute-done((f32[512,512]{0,1:T(8,128)}, f32[512,512]{0,1:T(8,128)}, u32[]{:S(2)}, u32[]{:S(2)}) %collective-permute-start.5) | collective-permute-done | bytes 1048608 | tf_op jit(solution)/shard_map/ppermute | solution.py:15
  374.3 11.8 %collective-permute-done.7 = f32[512,512]{1,0:T(8,128)} collective-permute-done((f32[512,512]{1,0:T(8,128)}, f32[512,512]{1,0:T(8,128)}, u32[]{:S(2)}, u32[]{:S(2)}) %collective-permute-start.7) | collective-permute-done | bytes 1048608 | tf_op jit(solution)/shard_map/ppermute | solution.py:15
  391.0 8.8 reduce-scatter.12.cloned.1.call-start
  399.8 10.5 %fusion.61 = f32[512,2048]{1,0:T(8,128)} fusion(bf16[512,2048]{1,0:T(8,128)(2,1)} %all-gather.9.cloned.1.call-done, bf16[2048,2048]{1,0:T(8,128)(2,1)} %all-gather.15.cloned.1.call-done), kind=kOutput, calls=%fused_computation.123 | convolution fusion | flops 4294967296 | bytes 14680064 | tf_op jit(solution)/shard_map/dot_general | solution.py:169
  410.4 9.8 all-gather.17.cloned.1.call-done
  420.2 12.2 %convert_reduce_fusion = (f32[2048]{0:T(1024)S(1)}, bf16[512,2048]{1,0:T(8,128)(2,1)S(1)}) fusion(f32[512,2048]{1,0:T(8,128)} %fusion.61, f32[2048]{0:T(1024)S(1)} %bitcast.106, bf16[512,2048]{1,0:T(8,128)(2,1)} %all-gather.19.cloned.1.call-done, bf16[2048,2048]{1,0:T(8,128)(2,1)} %all-gather.17.cloned.1.call-done), kind=kOutput, calls=%fused_computation.22 | convolution fusion | flops 4319082496 | bytes 16793600 | tf_op jit(solution)/shard_map/td,fd->tf/dot_general | solution.py:201
  446.0 11.6 %fusion.27 = bf16[8,64,512]{2,1,0:T(8,128)(2,1)S(1)} fusion(bf16[1536,8,64]{0,2,1:T(8,128)(2,1)S(1)} %bitcast.83, f32[8,512,1536]{2,1,0:T(8,128)} %get-tuple-element.268, f32[8,512]{1,0:T(8,128)S(1)} %copy-done.19, f32[8,512]{1,0:T(8,128)S(1)} %get-tuple-element.267, pred[512,1536]{1,0:T(8,128)(4,1)S(1)} %get-tuple-element.236), kind=kOutput, calls=%fused_computation.51 | convolution fusion | flops 837025792 | bytes 28082176 | tf_op jit(solution)/shard_map/while/body/eval_jaxpr/hqk,khe->qhe/dot_general | solution.py:164
  457.6 8.1 fusion.54
  470.3 8.0 convolution_bitcast_fusion
  483.5 12.6 %fusion.64 = f32[2048,2048]{1,0:T(8,128)} fusion(bf16[512,2048]{1,0:T(8,128)(2,1)} %all-gather.9.cloned.1.call-done, bf16[512,2048]{1,0:T(8,128)(2,1)} %copy-done.37), kind=kOutput, calls=%fused_computation.126 | convolution fusion | flops 4294967296 | bytes 20971520 | tf_op jit(solution)/shard_map/td,tf->df/dot_general | solution.py:206
  496.1 11.9 %fusion.53 = f32[2048,2048]{1,0:T(8,128)} fusion(bf16[512,2048]{1,0:T(8,128)(2,1)S(1)} %copy-done.11, f32[512,2048]{1,0:T(8,128)} %fusion.61, f32[2048]{0:T(1024)S(1)} %bitcast.108), kind=kOutput, calls=%fused_computation.116 | convolution fusion | flops 4305453056 | bytes 23076864 | tf_op jit(solution)/shard_map/tf,td->fd/dot_general | solution.py:200
  511.4 14.1 %all-reduce.9 = f32[2048]{0:T(1024)S(1)} all-reduce(f32[2048]{0:T(1024)S(1)} %get-tuple-element.233), channel_id=11, replica_groups=mesh['fsdp'=8,'tp'=4] {'fsdp'}, use_global_device_ids=true, to_apply=%region_23.24.clone | all-reduce | flops 2048 | bytes 16384
  526.1 10.6 %reduce-scatter.12.cloned.1.call-done = f32[128,2048]{1,0:T(8,128)} async-done(((f32[512,2048]{1,0:T(8,128)}), f32[128,2048]{1,0:T(8,128)}) %reduce-scatter.12.cloned.1.call-update) | async-done | bytes 1048592 | tf_op jit(solution)/shard_map/reduce_scatter | solution.py:268
  540.0 76.3 %reduce-scatter.10.cloned.1.call-done = f32[128,2048]{1,0:T(8,128)} async-done(((f32[512,2048]{1,0:T(8,128)}), f32[128,2048]{1,0:T(8,128)}) %reduce-scatter.10.cloned.1.call-update) | async-done | bytes 1048592 | tf_op jit(solution)/shard_map/reduce_scatter | solution.py:189
  619.5 41.2 %all-reduce.10 = (f32[2048]{0:T(1024)S(1)}, f32[2048]{0:T(1024)S(1)}, f32[2048]{0:T(1024)S(1)}) all-reduce(f32[2048]{0:T(1024)S(1)} %get-tuple-element.222, f32[2048]{0:T(1024)S(1)} %get-tuple-element.224, f32[2048]{0:T(1024)S(1)} %get-tuple-element.253), channel_id=4, replica_groups=mesh['fsdp'=8,'tp'=4] {'fsdp','tp'}, use_global_device_ids=true, to_apply=%region_12.13.clone | all-reduce | flops 6144 | bytes 49152
  661.9 51.6 %reduce-scatter.14.cloned.1.call-done = f32[3,256,512]{1,2,0:T(8,128)} async-done(((f32[3,2048,512]{1,2,0:T(8,128)}), f32[3,256,512]{1,2,0:T(8,128)}) %reduce-scatter.14.cloned.1.call-update) | async-done | bytes 1572880 | tf_op jit(solution)/shard_map/reduce_scatter | solution.py:273
  716.6 52.6 %reduce-scatter.16.cloned.1.call-done = f32[512,256]{1,0:T(8,128)} async-done(((f32[512,2048]{1,0:T(8,128)}), f32[512,256]{1,0:T(8,128)}) %reduce-scatter.16.cloned.1.call-update) | async-done | bytes 524304 | tf_op jit(solution)/shard_map/reduce_scatter | solution.py:275
  769.2 120.0 %reduce-scatter.18.cloned.1.call-done = f32[256,2048]{1,0:T(8,128)} async-done(((f32[2048,2048]{1,0:T(8,128)}), f32[256,2048]{1,0:T(8,128)}) %reduce-scatter.18.cloned.1.call-update) | async-done | bytes 2097168 | tf_op jit(solution)/shard_map/reduce_scatter | solution.py:276
  889.2 120.2 %reduce-scatter.20.cloned.1.call-done = f32[2048,256]{1,0:T(8,128)} async-done(((f32[2048,2048]{1,0:T(8,128)}), f32[2048,256]{1,0:T(8,128)}) %reduce-scatter.20.cloned.1.call-update) | async-done | bytes 2097168 | tf_op jit(solution)/shard_map/reduce_scatter | solution.py:278
  (198 shorter events, 117.2 us)
Async XLA Ops:
  7.2 56.0 %copy-start.21 = (s32[4096]{0:T(1024)S(1)}, s32[4096]{0:T(1024)}, u32[]{:S(2)}) copy-start(s32[4096]{0:T(1024)} %param.27) | copy-start | bytes 49156
  7.2 56.1 %copy-start.20 = (s32[4096]{0:T(1024)S(1)}, s32[4096]{0:T(1024)}, u32[]{:S(2)}) copy-start(s32[4096]{0:T(1024)} %param.29) | copy-start | bytes 49156
  7.2 56.3 %copy-start.29 = (s32[39,3]{0,1:T(4,128)S(1)}, s32[39,3]{0,1:T(4,128)}, u32[]{:S(2)}) copy-start(s32[39,3]{0,1:T(4,128)} %param.28) | copy-start | bytes 1408
  7.2 97.6 %all-gather.9.cloned.1.call-start = ((), (), s32[]{:S(2)}) async-start(), calls=%async_computation.7 | async-start | bytes 2621440 | tf_op jit(solution)/shard_map/all_gather | solution.py:136
  58.3 94.3 %all-gather.11.cloned.1.call-start = ((), (), s32[]{:S(2)}) async-start(), calls=%async_computation.8 | async-start | bytes 7077888 | tf_op jit(solution)/shard_map/all_gather | solution.py:129
  60.7 139.5 %all-gather.19.cloned.1.call-start = ((), (), s32[]{:S(2)}) async-start(), calls=%async_computation.13 | async-start | bytes 2621440 | tf_op jit(solution)/shard_map/all_gather | solution.py:192
  61.4 167.5 %all-gather.13.cloned.1.call-start = ((), (), s32[]{:S(2)}) async-start(), calls=%async_computation.9 | async-start | bytes 2359296 | tf_op jit(solution)/shard_map/all_gather | solution.py:131
  62.0 337.9 %all-gather.15.cloned.1.call-start = ((), (), s32[]{:S(2)}) async-start(), calls=%async_computation.10 | async-start | bytes 9437184 | tf_op jit(solution)/shard_map/all_gather | solution.py:132
  62.6 357.7 %all-gather.17.cloned.1.call-start = ((), (), s32[]{:S(2)}) async-start(), calls=%async_computation.11 | async-start | bytes 9437184 | tf_op jit(solution)/shard_map/all_gather | solution.py:134
  63.1 446.8 %reduce-scatter.22.cloned.1.call-start = ((), (), s32[]{:S(2)}) async-start(), calls=%async_computation.19 | async-start | bytes 294912
  160.5 78.9 %copy-start.14 = (bf16[512,8,64]{0,2,1:T(8,128)(2,1)}, bf16[512,8,64]{0,2,1:T(8,128)(2,1)S(1)}, u32[]{:S(2)}) copy-start(bf16[512,8,64]{0,2,1:T(8,128)(2,1)S(1)} %maximum_convert_fusion) | copy-start | bytes 1572868
  160.6 78.8 %collective-permute-start.2 = (bf16[512,512]{0,1:T(8,128)(2,1)S(1)}, bf16[512,512]{0,1:T(8,128)(2,1)}, u32[]{:S(2)}, u32[]{:S(2)}) collective-permute-start(bf16[512,512]{0,1:T(8,128)(2,1)S(1)} %bitcast.97), channel_id=1, source_target_pairs={{0,8},{4,12},{8,16},{12,20},{16,24},{20,28},{1,9},{5,13},{9,17},{1... | collective-permute-start | bytes 1572872 | tf_op jit(solution)/shard_map/ppermute | solution.py:15
  164.7 74.7 %collective-permute-start.3 = (bf16[512,512]{0,1:T(8,128)(2,1)S(1)}, bf16[512,512]{0,1:T(8,128)(2,1)}, u32[]{:S(2)}, u32[]{:S(2)}) collective-permute-start(bf16[512,512]{0,1:T(8,128)(2,1)S(1)} %bitcast.98), channel_id=1, source_target_pairs={{0,4},{4,8},{8,12},{12,16},{16,20},{20,24},{24,28},{1,5},{5,9},{9,... | collective-permute-start | bytes 1572872 | tf_op jit(solution)/shard_map/ppermute | solution.py:15
  233.8 29.2 %collective-permute-start = (bf16[512,512]{0,1:T(8,128)(2,1)S(1)}, bf16[512,512]{0,1:T(8,128)(2,1)S(1)}, u32[]{:S(2)}, u32[]{:S(2)}) collective-permute-start(bf16[512,512]{0,1:T(8,128)(2,1)S(1)} %fusion.41), channel_id=1, source_target_pairs={{0,8},{4,12},{8,16},{12,20},{16,24},{20,28},{1,9},{5,13},{9,17},{1... | collective-permute-start | bytes 1572872 | tf_op jit(solution)/shard_map/ppermute | solution.py:15
  237.2 25.8 %collective-permute-start.1 = (bf16[512,512]{0,1:T(8,128)(2,1)S(1)}, bf16[512,512]{0,1:T(8,128)(2,1)S(1)}, u32[]{:S(2)}, u32[]{:S(2)}) collective-permute-start(bf16[512,512]{0,1:T(8,128)(2,1)S(1)} %fusion.41), channel_id=1, source_target_pairs={{0,4},{4,8},{8,12},{12,16},{16,20},{20,24},{24,28},{1,5},{5,9},{9,... | collective-permute-start | bytes 1572872 | tf_op jit(solution)/shard_map/ppermute | solution.py:15
  307.2 33.2 %collective-permute-start.4 = (f32[512,512]{0,1:T(8,128)}, f32[512,512]{0,1:T(8,128)}, u32[]{:S(2)}, u32[]{:S(2)}) collective-permute-start(f32[512,512]{0,1:T(8,128)} %bitcast.23), channel_id=1, source_target_pairs={{4,0},{8,4},{12,8},{16,12},{20,16},{24,20},{28,24},{5,1},{9,5},{13... | collective-permute-start | bytes 3145736 | tf_op jit(solution)/shard_map/ppermute | solution.py:15
  308.5 54.5 %collective-permute-start.5 = (f32[512,512]{0,1:T(8,128)}, f32[512,512]{0,1:T(8,128)}, u32[]{:S(2)}, u32[]{:S(2)}) collective-permute-start(f32[512,512]{0,1:T(8,128)} %bitcast.24), channel_id=1, source_target_pairs={{8,0},{12,4},{16,8},{20,12},{24,16},{28,20},{9,1},{13,5},{17,9},{2... | collective-permute-start | bytes 3145736 | tf_op jit(solution)/shard_map/ppermute | solution.py:15
  324.9 49.4 %collective-permute-start.6 = (f32[512,512]{1,0:T(8,128)}, f32[512,512]{1,0:T(8,128)}, u32[]{:S(2)}, u32[]{:S(2)}) collective-permute-start(f32[512,512]{1,0:T(8,128)} %copy.71), channel_id=1, source_target_pairs={{4,0},{8,4},{12,8},{16,12},{20,16},{24,20},{28,24},{5,1},{9,5},{13... | collective-permute-start | bytes 3145736 | tf_op jit(solution)/shard_map/ppermute | solution.py:15
  327.5 58.6 %collective-permute-start.7 = (f32[512,512]{1,0:T(8,128)}, f32[512,512]{1,0:T(8,128)}, u32[]{:S(2)}, u32[]{:S(2)}) collective-permute-start(f32[512,512]{1,0:T(8,128)} %copy.73), channel_id=1, source_target_pairs={{8,0},{12,4},{16,8},{20,12},{24,16},{28,20},{9,1},{13,5},{17,9},{2... | collective-permute-start | bytes 3145736 | tf_op jit(solution)/shard_map/ppermute | solution.py:15
  391.0 29.2 %copy-start.24 = (f32[8,1,256]{2,1,0:T(1,128)S(1)}, f32[8,1,256]{2,1,0:T(1,128)}, u32[]{:S(2)}) copy-start(f32[8,1,256]{2,1,0:T(1,128)} %convert_element_type.155) | copy-start | bytes 24580
  391.0 145.7 %reduce-scatter.12.cloned.1.call-start = ((), (), s32[]{:S(2)}) async-start(), calls=%async_computation.14 | async-start | bytes 5242880 | tf_op jit(solution)/shard_map/reduce_scatter | solution.py:268
  445.3 171.0 %reduce-scatter.10.cloned.1.call-start = ((), (), s32[]{:S(2)}) async-start(), calls=%async_computation.12 | async-start | bytes 5242880 | tf_op jit(solution)/shard_map/reduce_scatter | solution.py:189
  469.1 244.5 %reduce-scatter.14.cloned.1.call-start = ((), (), s32[]{:S(2)}) async-start(), calls=%async_computation.15 | async-start | bytes 14155776 | tf_op jit(solution)/shard_map/reduce_scatter | solution.py:273
  478.3 290.9 %reduce-scatter.16.cloned.1.call-start = ((), (), s32[]{:S(2)}) async-start(), calls=%async_computation.16 | async-start | bytes 4718592 | tf_op jit(solution)/shard_map/reduce_scatter | solution.py:275
  483.2 406.1 %reduce-scatter.18.cloned.1.call-start = ((), (), s32[]{:S(2)}) async-start(), calls=%async_computation.17 | async-start | bytes 18874368 | tf_op jit(solution)/shard_map/reduce_scatter | solution.py:276
  496.1 513.3 %reduce-scatter.20.cloned.1.call-start = ((), (), s32[]{:S(2)}) async-start(), calls=%async_computation.18 | async-start | bytes 18874368 | tf_op jit(solution)/shard_map/reduce_scatter | solution.py:278
  508.0 28.7 %copy-start.1 = (bf16[128,2048]{1,0:T(8,128)(2,1)S(1)}, bf16[128,2048]{1,0:T(8,128)(2,1)}, u32[]{:S(2)}) copy-start(bf16[128,2048]{1,0:T(8,128)(2,1)} %param.15) | copy-start | bytes 1572868
  508.0 28.7 %copy-start.17 = (f32[2048]{0:T(1024)S(1)}, f32[2048]{0:T(1024)}, u32[]{:S(2)}) copy-start(f32[2048]{0:T(1024)} %copy-done.16) | copy-start | bytes 24580
  508.0 30.2 %copy-start.32 = (f32[128]{0:T(128)S(1)}, f32[128]{0:T(128)}, u32[]{:S(2)}) copy-start(f32[128]{0:T(128)} %copy-done.31) | copy-start | bytes 1540
  508.0 30.2 %copy-start.26 = (f32[128]{0:T(128)S(1)}, f32[128]{0:T(128)}, u32[]{:S(2)}) copy-start(f32[128]{0:T(128)} %copy-done.25) | copy-start | bytes 1540
  508.1 108.2 %copy-start.12 = (bf16[128,2048]{1,0:T(8,128)(2,1)S(1)}, bf16[128,2048]{1,0:T(8,128)(2,1)}, u32[]{:S(2)}) copy-start(bf16[128,2048]{1,0:T(8,128)(2,1)} %param.26) | copy-start | bytes 1572868
  660.7 349.2 %copy-start.36 = (f32[64]{0:T(128)}, f32[64]{0:T(128)S(1)}, u32[]{:S(2)}) copy-start(f32[64]{0:T(128)S(1)} %dynamic-slice.2) | copy-start | bytes 772
  (28 other events, 196.8 us)
Sparse Core Ops, SparseCore 0:
  58.4 46.3 all-gather.8
  107.2 45.3 all-gather.10
  154.2 45.9 all-gather.18
  201.9 26.8 all-gather.12
  230.6 64.4 all-gather.14
  296.8 123.3 all-gather.16
  423.8 33.6 reduce-scatter.21
  459.9 76.7 reduce-scatter.11
  539.0 77.2 reduce-scatter.9
  620.0 93.4 reduce-scatter.13
  717.9 51.3 reduce-scatter.15
  773.2 115.9 reduce-scatter.17
  893.4 115.9 reduce-scatter.19
where the time goes:
time: 1020 us
  waiting for transfers between devices  607 us (60%)
  matrix products  158 us (15%)
  blocking collectives  116 us (11%)
  other arithmetic  54 us (5%)
  local copies, waits for them, and re-layouts  40 us (4%)
  starting transfers between devices  27.1 us (3%)
  between operations  15.8 us (2%)
    reduce_scatter x1, waiting for transfers between devices, body(): lax.psum_scatter(outer_grad, 'fsdp', scatter_dimension=1, tiled=True)  120 us
    reduce_scatter x1, waiting for transfers between devices, body(): lax.psum_scatter(inner_grad, 'fsdp', scatter_dimension=0, tiled=True)  120 us
    unnamed x3, blocking collectives  97.5 us
    reduce_scatter x1, waiting for transfers between devices, body(): lax.psum_scatter(partial_rows, 'tp', scatter_dimension=0, tiled=True)  76.3 us
    reduce_scatter x1, waiting for transfers between devices, body(): lax.psum_scatter(dense_grad, 'fsdp', scatter_dimension=1, tiled=True)  52.6 us
    reduce_scatter x1, waiting for transfers between devices, body(): lax.psum_scatter(qkv_weight_part, 'fsdp', scatter_dimension=1, tiled=True)  51.6 us
    all_gather x1, waiting for transfers between devices, forward_pieces(): lax.all_gather(qkv_weight, 'fsdp', axis=1, tiled=True)  47.9 us
    ppermute x8, waiting for transfers between devices, passed_along(): lax.ppermute(value, axis, [(source, source + steps) for source in range(i...  34.4 us
  transfers between devices with their start and end apart: 21, of which 13 were waited for; matrix products, arithmetic and copies ran while one was open for 23% of the time, Pallas kernels for 0%

commit v1 on v0

--- a/solution.py
+++ b/solution.py
@@ -7,6 +7,30 @@
 ROTARY = 32
 TREE_LEN = 1024
 EPSILON = 1e-05
+
+
+def pools_report(my_tile):
+    wide_out, v_now, inter = (lax.axis_size("fsdp"), lax.axis_index("fsdp"), my_tile.shape[1])
+    pool = [it * wide_out if jj == 1 else it for jj, it in enumerate(my_tile.shape)]
+    mixed_arr = lax.dynamic_update_slice_in_dim(
+        jnp.zeros(pool, my_tile.dtype), my_tile, v_now * inter, axis=1
+    )
+    reached = all_values = my_tile
+    for i in range(1, wide_out // 2 + 1):
+        reached = lax.ppermute(
+            reached, "fsdp", list(map(lambda jj: (jj, (jj + 1) % wide_out), range(wide_out)))
+        )
+        mixed_arr = lax.dynamic_update_slice_in_dim(
+            mixed_arr, reached, (v_now - i) % wide_out * inter, axis=1
+        )
+        if 2 * i < wide_out:
+            all_values = lax.ppermute(
+                all_values, "fsdp", list(map(lambda jj: (jj, (jj - 1) % wide_out), range(wide_out)))
+            )
+            mixed_arr = lax.dynamic_update_slice_in_dim(
+                mixed_arr, all_values, (v_now + i) % wide_out * inter, axis=1
+            )
+    return mixed_arr
 
 
 def passed_along(value, axis, steps):
@@ -126,7 +150,7 @@
 
     def forward_pieces():
         gathered = (
-            lax.all_gather(qkv_weight, "fsdp", axis=1, tiled=True),
+            pools_report(qkv_weight),
             lax.all_gather(qkv_bias, "fsdp", axis=1, tiled=True),
             lax.all_gather(dense_weight, "fsdp", axis=1, tiled=True),
             lax.all_gather(inner_weight, "fsdp", axis=0, tiled=True),

time: 1020 us -> 965 us (0.946)
  waiting for transfers between devices: 607 us -> 522 us
  blocking collectives: 116 us -> 133 us
    all_gather x1 -> x0, waiting for transfers between devices: 47.9 us -> none  [forward_pieces(): lax.all_gather(qkv_weight, 'fsdp', axis=1, tiled=True)]
    all_gather x1, waiting for transfers between devices: 32.8 us -> 0.02 us  [body(): grad_rows = lax.all_gather(cotangent, 'tp', axis=0, tiled=True)]
    ppermute x0 -> x7, waiting for transfers between devices: none -> 31.7 us  [the longest x4 31.6 us: pools_report(): lax.ppermute(reached, 'fsdp', list(map(lambda jj: (jj, (jj + 1) % wide_ou...]
    all_gather x1, waiting for transfers between devices: 28.7 us -> 0.02 us  [forward_pieces(): lax.all_gather(dense_weight, 'fsdp', axis=1, tiled=True)]
    all_gather x1, waiting for transfers between devices: 19.4 us -> 0.01 us  [forward_pieces(): normed = lax.all_gather(normed_local, 'tp', axis=0, tiled=True)]
    all_gather x1, blocking collectives: 10.2 us -> 20.7 us  [forward_pieces(): lax.all_gather(qkv_bias, 'fsdp', axis=1, tiled=True)]
    unnamed x97 -> x98, local copies, waits for them, and re-layouts: 23.9 us -> 20.3 us
  transfers between devices with their start and end apart: 21 -> 27, of which waited for: 13 -> 13; matrix products, arithmetic and copies ran while one was open for 23% -> 25% of each run, Pallas kernels for 0% -> 0%
where the time goes in v1:
time: 965 us; the launch traced here: 956 us
  waiting for transfers between devices  522 us (54%)
  matrix products  160 us (17%)
  blocking collectives  133 us (14%)
  other arithmetic  54.1 us (6%)
  local copies, waits for them, and re-layouts  47.1 us (5%)
  starting transfers between devices  24.9 us (3%)
  between operations  16.1 us (2%)
    reduce_scatter x1, waiting for transfers between devices, body(): lax.psum_scatter(inner_grad, 'fsdp', scatter_dimension=0, tiled=True)  120 us
    reduce_scatter x1, waiting for transfers between devices, body(): lax.psum_scatter(outer_grad, 'fsdp', scatter_dimension=1, tiled=True)  120 us
    unnamed x3, blocking collectives  97.5 us
    reduce_scatter x1, waiting for transfers between devices, body(): lax.psum_scatter(partial_rows, 'tp', scatter_dimension=0, tiled=True)  76.3 us
    reduce_scatter x1, waiting for transfers between devices, body(): lax.psum_scatter(dense_grad, 'fsdp', scatter_dimension=1, tiled=True)  52.5 us
    reduce_scatter x1, waiting for transfers between devices, body(): lax.psum_scatter(qkv_weight_part, 'fsdp', scatter_dimension=1, tiled=True)  51.8 us
    ppermute x8, waiting for transfers between devices, passed_along(): lax.ppermute(value, axis, [(source, source + steps) for source in range(i...  40.7 us
    ppermute x4, waiting for transfers between devices, pools_report(): lax.ppermute(reached, 'fsdp', list(map(lambda jj: (jj, (jj + 1) % wide_ou...  31.6 us
  transfers between devices with their start and end apart: 27, of which 13 were waited for; matrix products, arithmetic and copies ran while one was open for 25% of the time, Pallas kernels for 0%

profile of v1, /device:TPU:0, one launch (start us, length us, event | category | flops | bytes accessed | tf_op | source)
XLA Modules:
  0.0 956.4 jit_solution(10730499948898639781)
XLA Ops:
  10.8 42.2 %all-reduce.11 = (bf16[2048]{0:T(1024)(128)(2,1)S(1)}, bf16[2048]{0:T(1024)(128)(2,1)S(1)}, bf16[2048]{0:T(1024)(128)(2,1)}, bf16[2048]{0:T(1024)(128)(2,1)}) all-reduce(bf16[2048]{0:T(1024)(128)(2,1)S(1)} %dynamic-update-slice.1, bf16[2048]{0:T(1024)(128)(2,1)S(1)} %dynamic-update-slice, ...), channel_id=1, replica_groups=mesh['fsdp'=8,'tp'=4] {'fsdp','tp'}, use_global_device_ids=true, to_apply=%add.3 | all-reduce | flops 8192 | bytes 32768
  62.7 20.7 %all-gather = bf16[8,64,3]{1,2,0:T(4,128)(2,1)S(1)} all-gather(bf16[1,64,3]{1,2,0:T(4,128)(2,1)S(1)} %bitcast.110), channel_id=1, replica_groups=mesh['fsdp'=8,'tp'=4] {'fsdp'}, dimensions={0}, use_global_device_ids=true | all-gather | bytes 3456 | tf_op jit(solution)/shard_map/all_gather | solution.py:154
  88.5 13.9 %collective-permute-done.2 = bf16[3,256,512]{2,1,0:T(8,128)(2,1)S(1)} collective-permute-done((bf16[3,256,512]{2,1,0:T(8,128)(2,1)S(1)}, bf16[3,256,512]{2,1,0:T(8,128)(2,1)S(1)}, u32[]{:S(2)}, u32[]{:S(2)}) %collective-permute-start.2) | collective-permute-done | bytes 786464 | tf_op jit(solution)/shard_map/ppermute | solution.py:20
  110.3 11.0 %collective-permute-done.4 = bf16[3,256,512]{2,1,0:T(8,128)(2,1)S(1)} collective-permute-done((bf16[3,256,512]{2,1,0:T(8,128)(2,1)S(1)}, bf16[3,256,512]{2,1,0:T(8,128)(2,1)S(1)}, u32[]{:S(2)}, u32[]{:S(2)}) %collective-permute-start.4) | collective-permute-done | bytes 786464 | tf_op jit(solution)/shard_map/ppermute | solution.py:20
  127.1 6.6 collective-permute-done.6
  134.7 6.3 add_bitcast_fusion
  146.9 14.4 %all-gather.1 = bf16[8,1,256]{2,1,0:T(2,128)(2,1)S(1)} all-gather(bf16[1,1,256]{2,1,0:T(2,128)(2,1)S(1)} %reshape.435), channel_id=1, replica_groups=mesh['fsdp'=8,'tp'=4] {'fsdp'}, dimensions={0}, use_global_device_ids=true | all-gather | bytes 4608 | tf_op jit(solution)/shard_map/all_gather | solution.py:157
  169.4 12.0 %select_reduce_fusion = (f32[8,512]{1,0:T(8,128)S(1)}, f32[8,512,1536]{2,1,0:T(8,128)}) fusion(pred[512,1536]{1,0:T(8,128)(4,1)S(1)} %get-tuple-element.236, bf16[512,8,64]{0,2,1:T(8,128)(2,1)S(1)} %maximum_convert_fusion, bf16[512,8,64]{0,2,1:T(8,128)(2,1)} %bitcast.14, bf16[512,8,64]{0,2,1:T(8,128)(2,1)} %bitcast.13, bf16[512,8,32]{0,2,1:T(8,128)(2,1)S(1)} %slice.202, ...), kind=kOutput, calls=%fused_computation.5 | convolution fusion | flops 830468096 | bytes 28065792 | tf_op jit(solution)/shard_map/while/body/eval_jaxpr/qhe,khe->hqk/dot_general | solution.py:181
  181.4 11.6 %fusion = f32[8,512]{1,0:T(8,128)S(1)} fusion(f32[8,512,1536]{2,1,0:T(8,128)} %get-tuple-element.268, f32[8,512]{1,0:T(8,128)S(1)} %get-tuple-element.267, pred[512,1536]{1,0:T(8,128)(4,1)S(1)} %get-tuple-element.236), kind=kLoop, calls=%fused_computation.6 | loop fusion | flops 25161728 | bytes 25985024 | tf_op jit(solution)/shard_map/while/body/eval_jaxpr/reduce_sum | solution.py:186
  197.2 20.0 %multiply_reduce_fusion = (f32[8,512]{1,0:T(8,128)S(1)}, f32[8,512,1536]{2,1,0:T(8,128)}) fusion(f32[8,512,1536]{2,1,0:T(8,128)} %get-tuple-element.268, f32[8,512]{1,0:T(8,128)S(1)} %log_add_fusion, pred[512,1536]{1,0:T(8,128)(4,1)S(1)} %get-tuple-element.236, bf16[512,8,64]{0,2,1:T(8,128)(2,1)S(1)} %bitcast.100, bf16[1536,8,64]{0,2,1:T(8,128)(2,1)S(1)} %bitcast.82), kind=kOutput, calls=%fused_computation.1 | convolution fusion | flops 836759552 | bytes 53248000 | tf_op jit(solution)/shard_map/while/body/eval_jaxpr/qhe,khe->hqk/dot_general | solution.py:246
  217.2 17.4 %multiply_convert_fusion = bf16[8,512,1536]{2,1,0:T(8,128)(2,1)S(1)} fusion(f32[8,512,1536]{2,1,0:T(8,128)} %get-tuple-element.270, f32[8,512,1536]{2,1,0:T(8,128)} %get-tuple-element.268, f32[8,512]{1,0:T(8,128)S(1)} %get-tuple-element.269, f32[8,512]{1,0:T(8,128)S(1)} %log_add_fusion, pred[512,1536]{1,0:T(8,128)(4,1)S(1)} %get-tuple-element.236), kind=kLoop, calls=%fused_computation | loop fusion | flops 37748736 | bytes 63733760 | tf_op jit(solution)/shard_map/while/body/eval_jaxpr/convert_element_type | solution.py:248
  243.9 11.8 %fusion.14 = f32[1536,8,64]{0,2,1:T(8,128)S(1)} fusion(bf16[512,8,64]{0,2,1:T(8,128)(2,1)S(1)} %bitcast.101, f32[8,512,1536]{2,1,0:T(8,128)} %get-tuple-element.268, f32[8,512]{1,0:T(8,128)S(1)} %log_add_fusion, pred[512,1536]{1,0:T(8,128)(4,1)S(1)} %get-tuple-element.236), kind=kOutput, calls=%fused_computation.26 | convolution fusion | flops 830472192 | bytes 29638656 | tf_op jit(solution)/shard_map/while/body/eval_jaxpr/hqk,qhe->khe/dot_general | solution.py:256
  263.7 9.0 fusion.26
  275.3 28.1 %collective-permute-done.12 = f32[512,512]{0,1:T(8,128)} collective-permute-done((f32[512,512]{0,1:T(8,128)}, f32[512,512]{0,1:T(8,128)}, u32[]{:S(2)}, u32[]{:S(2)}) %collective-permute-start.12) | collective-permute-done | bytes 1048608 | tf_op jit(solution)/shard_map/ppermute | solution.py:39
  314.7 12.6 %collective-permute-done.14 = f32[512,512]{1,0:T(8,128)} collective-permute-done((f32[512,512]{1,0:T(8,128)}, f32[512,512]{1,0:T(8,128)}, u32[]{:S(2)}, u32[]{:S(2)}) %collective-permute-start.14) | collective-permute-done | bytes 1048608 | tf_op jit(solution)/shard_map/ppermute | solution.py:39
  332.5 10.9 %fusion.61 = f32[512,2048]{1,0:T(8,128)} fusion(bf16[512,2048]{1,0:T(8,128)(2,1)} %all-gather.8.cloned.1.call-done, bf16[2048,2048]{1,0:T(8,128)(2,1)} %all-gather.12.cloned.1.call-done), kind=kOutput, calls=%fused_computation.131 | convolution fusion | flops 4294967296 | bytes 14680064 | tf_op jit(solution)/shard_map/dot_general | solution.py:193
  343.5 16.1 %all-gather.14.cloned.1.call-done = bf16[2048,2048]{1,0:T(8,128)(2,1)} async-done(((bf16[2048,256]{1,0:T(8,128)(2,1)}), bf16[2048,2048]{1,0:T(8,128)(2,1)}) %all-gather.14.cloned.1.call-update) | async-done | bytes 8388624 | tf_op jit(solution)/shard_map/all_gather | solution.py:158
  359.6 12.2 %convert_reduce_fusion = (f32[2048]{0:T(1024)S(1)}, bf16[512,2048]{1,0:T(8,128)(2,1)S(1)}) fusion(f32[512,2048]{1,0:T(8,128)} %fusion.61, f32[2048]{0:T(1024)S(1)} %bitcast.106, bf16[512,2048]{1,0:T(8,128)(2,1)} %all-gather.16.cloned.1.call-done, bf16[2048,2048]{1,0:T(8,128)(2,1)} %all-gather.14.cloned.1.call-done), kind=kOutput, calls=%fused_computation.22 | convolution fusion | flops 4319082496 | bytes 16793600 | tf_op jit(solution)/shard_map/td,fd->tf/dot_general | solution.py:225
  376.7 7.9 bitcast_add_fusion
  385.3 11.6 %fusion.27 = bf16[8,64,512]{2,1,0:T(8,128)(2,1)S(1)} fusion(bf16[1536,8,64]{0,2,1:T(8,128)(2,1)S(1)} %bitcast.83, f32[8,512,1536]{2,1,0:T(8,128)} %get-tuple-element.268, f32[8,512]{1,0:T(8,128)S(1)} %copy-done.20, f32[8,512]{1,0:T(8,128)S(1)} %get-tuple-element.267, pred[512,1536]{1,0:T(8,128)(4,1)S(1)} %get-tuple-element.236), kind=kOutput, calls=%fused_computation.51 | convolution fusion | flops 837025792 | bytes 28082176 | tf_op jit(solution)/shard_map/while/body/eval_jaxpr/hqk,khe->qhe/dot_general | solution.py:188
  397.0 8.1 fusion.54
  409.7 7.9 convolution_bitcast_fusion
  422.8 12.5 %fusion.64 = f32[2048,2048]{1,0:T(8,128)} fusion(bf16[512,2048]{1,0:T(8,128)(2,1)} %all-gather.8.cloned.1.call-done, bf16[512,2048]{1,0:T(8,128)(2,1)} %copy-done.38), kind=kOutput, calls=%fused_computation.134 | convolution fusion | flops 4294967296 | bytes 20971520 | tf_op jit(solution)/shard_map/td,tf->df/dot_general | solution.py:230
  435.4 12.1 %fusion.53 = f32[2048,2048]{1,0:T(8,128)} fusion(bf16[512,2048]{1,0:T(8,128)(2,1)S(1)} %copy-done.11, f32[512,2048]{1,0:T(8,128)} %fusion.61, f32[2048]{0:T(1024)S(1)} %bitcast.108), kind=kOutput, calls=%fused_computation.124 | convolution fusion | flops 4305453056 | bytes 23076864 | tf_op jit(solution)/shard_map/tf,td->fd/dot_general | solution.py:224
  450.9 14.1 %all-reduce.9 = f32[2048]{0:T(1024)S(1)} all-reduce(f32[2048]{0:T(1024)S(1)} %get-tuple-element.233), channel_id=11, replica_groups=mesh['fsdp'=8,'tp'=4] {'fsdp'}, use_global_device_ids=true, to_apply=%region_23.24.clone | all-reduce | flops 2048 | bytes 16384
  465.6 10.3 %reduce-scatter.12.cloned.1.call-done = f32[128,2048]{1,0:T(8,128)} async-done(((f32[512,2048]{1,0:T(8,128)}), f32[128,2048]{1,0:T(8,128)}) %reduce-scatter.12.cloned.1.call-update) | async-done | bytes 1048592 | tf_op jit(solution)/shard_map/reduce_scatter | solution.py:292
  479.3 76.3 %reduce-scatter.10.cloned.1.call-done = f32[128,2048]{1,0:T(8,128)} async-done(((f32[512,2048]{1,0:T(8,128)}), f32[128,2048]{1,0:T(8,128)}) %reduce-scatter.10.cloned.1.call-update) | async-done | bytes 1048592 | tf_op jit(solution)/shard_map/reduce_scatter | solution.py:213
  558.7 41.2 %all-reduce.10 = (f32[2048]{0:T(1024)S(1)}, f32[2048]{0:T(1024)S(1)}, f32[2048]{0:T(1024)S(1)}) all-reduce(f32[2048]{0:T(1024)S(1)} %get-tuple-element.222, f32[2048]{0:T(1024)S(1)} %get-tuple-element.224, f32[2048]{0:T(1024)S(1)} %get-tuple-element.253), channel_id=4, replica_groups=mesh['fsdp'=8,'tp'=4] {'fsdp','tp'}, use_global_device_ids=true, to_apply=%region_12.13.clone | all-reduce | flops 6144 | bytes 49152
  601.2 51.8 %reduce-scatter.14.cloned.1.call-done = f32[3,256,512]{1,2,0:T(8,128)} async-done(((f32[3,2048,512]{1,2,0:T(8,128)}), f32[3,256,512]{1,2,0:T(8,128)}) %reduce-scatter.14.cloned.1.call-update) | async-done | bytes 1572880 | tf_op jit(solution)/shard_map/reduce_scatter | solution.py:297
  656.0 52.5 %reduce-scatter.16.cloned.1.call-done = f32[512,256]{1,0:T(8,128)} async-done(((f32[512,2048]{1,0:T(8,128)}), f32[512,256]{1,0:T(8,128)}) %reduce-scatter.16.cloned.1.call-update) | async-done | bytes 524304 | tf_op jit(solution)/shard_map/reduce_scatter | solution.py:299
  708.5 120.1 %reduce-scatter.18.cloned.1.call-done = f32[256,2048]{1,0:T(8,128)} async-done(((f32[2048,2048]{1,0:T(8,128)}), f32[256,2048]{1,0:T(8,128)}) %reduce-scatter.18.cloned.1.call-update) | async-done | bytes 2097168 | tf_op jit(solution)/shard_map/reduce_scatter | solution.py:300
  828.6 120.0 %reduce-scatter.20.cloned.1.call-done = f32[2048,256]{1,0:T(8,128)} async-done(((f32[2048,2048]{1,0:T(8,128)}), f32[2048,256]{1,0:T(8,128)}) %reduce-scatter.20.cloned.1.call-update) | async-done | bytes 2097168 | tf_op jit(solution)/shard_map/reduce_scatter | solution.py:302
  (219 shorter events, 117.0 us)
Async XLA Ops:
  7.2 76.3 %copy-start.22 = (s32[4096]{0:T(1024)S(1)}, s32[4096]{0:T(1024)}, u32[]{:S(2)}) copy-start(s32[4096]{0:T(1024)} %param.27) | copy-start | bytes 49156
  7.2 76.3 %copy-start.21 = (s32[4096]{0:T(1024)S(1)}, s32[4096]{0:T(1024)}, u32[]{:S(2)}) copy-start(s32[4096]{0:T(1024)} %param.29) | copy-start | bytes 49156
  7.2 76.5 %copy-start.30 = (s32[39,3]{0,1:T(4,128)S(1)}, s32[39,3]{0,1:T(4,128)}, u32[]{:S(2)}) copy-start(s32[39,3]{0,1:T(4,128)} %param.28) | copy-start | bytes 1408
  7.2 127.4 %all-gather.8.cloned.1.call-start = ((), (), s32[]{:S(2)}) async-start(), calls=%async_computation.7 | async-start | bytes 2621440 | tf_op jit(solution)/shard_map/all_gather | solution.py:160
  57.8 135.4 %all-gather.16.cloned.1.call-start = ((), (), s32[]{:S(2)}) async-start(), calls=%async_computation.12 | async-start | bytes 2621440 | tf_op jit(solution)/shard_map/all_gather | solution.py:216
  58.6 134.6 %all-gather.10.cloned.1.call-start = ((), (), s32[]{:S(2)}) async-start(), calls=%async_computation.8 | async-start | bytes 2359296 | tf_op jit(solution)/shard_map/all_gather | solution.py:155
  59.3 273.2 %all-gather.12.cloned.1.call-start = ((), (), s32[]{:S(2)}) async-start(), calls=%async_computation.9 | async-start | bytes 9437184 | tf_op jit(solution)/shard_map/all_gather | solution.py:156
  59.9 299.7 %all-gather.14.cloned.1.call-start = ((), (), s32[]{:S(2)}) async-start(), calls=%async_computation.10 | async-start | bytes 9437184 | tf_op jit(solution)/shard_map/all_gather | solution.py:158
  60.0 24.0 %collective-permute-start = (bf16[3,256,512]{2,1,0:T(8,128)(2,1)S(1)}, bf16[3,256,512]{2,1,0:T(8,128)(2,1)S(1)}, u32[]{:S(2)}, u32[]{:S(2)}) collective-permute-start(bf16[3,256,512]{2,1,0:T(8,128)(2,1)S(1)} %copy-done.16), channel_id=1, source_target_pairs={{0,4},{4,8},{8,12},{12,16},{16,20},{20,24},{24,28},{28,0},{1,5},{5... | collective-permute-start | bytes 2359304 | tf_op jit(solution)/shard_map/ppermute | solution.py:20
  60.0 26.1 %collective-permute-start.1 = (bf16[3,256,512]{2,1,0:T(8,128)(2,1)S(1)}, bf16[3,256,512]{2,1,0:T(8,128)(2,1)S(1)}, u32[]{:S(2)}, u32[]{:S(2)}) collective-permute-start(bf16[3,256,512]{2,1,0:T(8,128)(2,1)S(1)} %copy-done.16), channel_id=1, source_target_pairs={{0,28},{4,0},{8,4},{12,8},{16,12},{20,16},{24,20},{28,24},{1,29},{... | collective-permute-start | bytes 2359304 | tf_op jit(solution)/shard_map/ppermute | solution.py:27
  83.9 18.5 %collective-permute-start.2 = (bf16[3,256,512]{2,1,0:T(8,128)(2,1)S(1)}, bf16[3,256,512]{2,1,0:T(8,128)(2,1)S(1)}, u32[]{:S(2)}, u32[]{:S(2)}) collective-permute-start(bf16[3,256,512]{2,1,0:T(8,128)(2,1)S(1)} %collective-permute-done), channel_id=1, source_target_pairs={{0,4},{4,8},{8,12},{12,16},{16,20},{20,24},{24,28},{28,0},{1,5},{5... | collective-permute-start | bytes 2359304 | tf_op jit(solution)/shard_map/ppermute | solution.py:20
  86.2 17.3 %collective-permute-start.3 = (bf16[3,256,512]{2,1,0:T(8,128)(2,1)S(1)}, bf16[3,256,512]{2,1,0:T(8,128)(2,1)S(1)}, u32[]{:S(2)}, u32[]{:S(2)}) collective-permute-start(bf16[3,256,512]{2,1,0:T(8,128)(2,1)S(1)} %collective-permute-done.1), channel_id=1, source_target_pairs={{0,28},{4,0},{8,4},{12,8},{16,12},{20,16},{24,20},{28,24},{1,29},{... | collective-permute-start | bytes 2359304 | tf_op jit(solution)/shard_map/ppermute | solution.py:27
  102.4 18.9 %collective-permute-start.4 = (bf16[3,256,512]{2,1,0:T(8,128)(2,1)S(1)}, bf16[3,256,512]{2,1,0:T(8,128)(2,1)S(1)}, u32[]{:S(2)}, u32[]{:S(2)}) collective-permute-start(bf16[3,256,512]{2,1,0:T(8,128)(2,1)S(1)} %collective-permute-done.2), channel_id=1, source_target_pairs={{0,4},{4,8},{8,12},{12,16},{16,20},{20,24},{24,28},{28,0},{1,5},{5... | collective-permute-start | bytes 2359304 | tf_op jit(solution)/shard_map/ppermute | solution.py:20
  103.5 22.6 %collective-permute-start.5 = (bf16[3,256,512]{2,1,0:T(8,128)(2,1)S(1)}, bf16[3,256,512]{2,1,0:T(8,128)(2,1)S(1)}, u32[]{:S(2)}, u32[]{:S(2)}) collective-permute-start(bf16[3,256,512]{2,1,0:T(8,128)(2,1)S(1)} %collective-permute-done.3), channel_id=1, source_target_pairs={{0,28},{4,0},{8,4},{12,8},{16,12},{20,16},{24,20},{28,24},{1,29},{... | collective-permute-start | bytes 2359304 | tf_op jit(solution)/shard_map/ppermute | solution.py:27
  121.4 12.3 %collective-permute-start.6 = (bf16[3,256,512]{2,1,0:T(8,128)(2,1)S(1)}, bf16[3,256,512]{2,1,0:T(8,128)(2,1)S(1)}, u32[]{:S(2)}, u32[]{:S(2)}) collective-permute-start(bf16[3,256,512]{2,1,0:T(8,128)(2,1)S(1)} %collective-permute-done.4), channel_id=1, source_target_pairs={{0,4},{4,8},{8,12},{12,16},{16,20},{20,24},{24,28},{28,0},{1,5},{5... | collective-permute-start | bytes 2359304 | tf_op jit(solution)/shard_map/ppermute | solution.py:20
  142.6 26.8 %collective-permute-start.9 = (bf16[512,512]{0,1:T(8,128)(2,1)S(1)}, bf16[512,512]{0,1:T(8,128)(2,1)}, u32[]{:S(2)}, u32[]{:S(2)}) collective-permute-start(bf16[512,512]{0,1:T(8,128)(2,1)S(1)} %bitcast.97), channel_id=1, source_target_pairs={{0,8},{4,12},{8,16},{12,20},{16,24},{20,28},{1,9},{5,13},{9,17},{1... | collective-permute-start | bytes 1572872 | tf_op jit(solution)/shard_map/ppermute | solution.py:39
  144.7 24.7 %collective-permute-start.10 = (bf16[512,512]{0,1:T(8,128)(2,1)S(1)}, bf16[512,512]{0,1:T(8,128)(2,1)}, u32[]{:S(2)}, u32[]{:S(2)}) collective-permute-start(bf16[512,512]{0,1:T(8,128)(2,1)S(1)} %bitcast.98), channel_id=1, source_target_pairs={{0,4},{4,8},{8,12},{12,16},{16,20},{20,24},{24,28},{1,5},{5,9},{9,... | collective-permute-start | bytes 1572872 | tf_op jit(solution)/shard_map/ppermute | solution.py:39
  146.9 302.6 %reduce-scatter.22.cloned.1.call-start = ((), (), s32[]{:S(2)}) async-start(), calls=%async_computation.18 | async-start | bytes 294912
  163.2 29.9 %collective-permute-start.7 = (bf16[512,512]{0,1:T(8,128)(2,1)S(1)}, bf16[512,512]{0,1:T(8,128)(2,1)S(1)}, u32[]{:S(2)}, u32[]{:S(2)}) collective-permute-start(bf16[512,512]{0,1:T(8,128)(2,1)S(1)} %fusion.41), channel_id=1, source_target_pairs={{0,8},{4,12},{8,16},{12,20},{16,24},{20,28},{1,9},{5,13},{9,17},{1... | collective-permute-start | bytes 1572872 | tf_op jit(solution)/shard_map/ppermute | solution.py:39
  167.2 25.9 %collective-permute-start.8 = (bf16[512,512]{0,1:T(8,128)(2,1)S(1)}, bf16[512,512]{0,1:T(8,128)(2,1)S(1)}, u32[]{:S(2)}, u32[]{:S(2)}) collective-permute-start(bf16[512,512]{0,1:T(8,128)(2,1)S(1)} %fusion.41), channel_id=1, source_target_pairs={{0,4},{4,8},{8,12},{12,16},{16,20},{20,24},{24,28},{1,5},{5,9},{9,... | collective-permute-start | bytes 1572872 | tf_op jit(solution)/shard_map/ppermute | solution.py:39
  240.9 34.4 %collective-permute-start.11 = (f32[512,512]{0,1:T(8,128)}, f32[512,512]{0,1:T(8,128)}, u32[]{:S(2)}, u32[]{:S(2)}) collective-permute-start(f32[512,512]{0,1:T(8,128)} %bitcast.23), channel_id=1, source_target_pairs={{4,0},{8,4},{12,8},{16,12},{20,16},{24,20},{28,24},{5,1},{9,5},{13... | collective-permute-start | bytes 3145736 | tf_op jit(solution)/shard_map/ppermute | solution.py:39
  242.2 61.2 %collective-permute-start.12 = (f32[512,512]{0,1:T(8,128)}, f32[512,512]{0,1:T(8,128)}, u32[]{:S(2)}, u32[]{:S(2)}) collective-permute-start(f32[512,512]{0,1:T(8,128)} %bitcast.24), channel_id=1, source_target_pairs={{8,0},{12,4},{16,8},{20,12},{24,16},{28,20},{9,1},{13,5},{17,9},{2... | collective-permute-start | bytes 3145736 | tf_op jit(solution)/shard_map/ppermute | solution.py:39
  259.8 54.9 %collective-permute-start.13 = (f32[512,512]{1,0:T(8,128)}, f32[512,512]{1,0:T(8,128)}, u32[]{:S(2)}, u32[]{:S(2)}) collective-permute-start(f32[512,512]{1,0:T(8,128)} %copy.67), channel_id=1, source_target_pairs={{4,0},{8,4},{12,8},{16,12},{20,16},{24,20},{28,24},{5,1},{9,5},{13... | collective-permute-start | bytes 3145736 | tf_op jit(solution)/shard_map/ppermute | solution.py:39
  262.4 64.9 %collective-permute-start.14 = (f32[512,512]{1,0:T(8,128)}, f32[512,512]{1,0:T(8,128)}, u32[]{:S(2)}, u32[]{:S(2)}) collective-permute-start(f32[512,512]{1,0:T(8,128)} %copy.69), channel_id=1, source_target_pairs={{8,0},{12,4},{16,8},{20,12},{24,16},{28,20},{9,1},{13,5},{17,9},{2... | collective-permute-start | bytes 3145736 | tf_op jit(solution)/shard_map/ppermute | solution.py:39
  332.3 143.7 %reduce-scatter.12.cloned.1.call-start = ((), (), s32[]{:S(2)}) async-start(), calls=%async_computation.13 | async-start | bytes 5242880 | tf_op jit(solution)/shard_map/reduce_scatter | solution.py:292
  384.6 170.9 %reduce-scatter.10.cloned.1.call-start = ((), (), s32[]{:S(2)}) async-start(), calls=%async_computation.11 | async-start | bytes 5242880 | tf_op jit(solution)/shard_map/reduce_scatter | solution.py:213
  408.5 244.4 %reduce-scatter.14.cloned.1.call-start = ((), (), s32[]{:S(2)}) async-start(), calls=%async_computation.14 | async-start | bytes 14155776 | tf_op jit(solution)/shard_map/reduce_scatter | solution.py:297
  417.7 290.8 %reduce-scatter.16.cloned.1.call-start = ((), (), s32[]{:S(2)}) async-start(), calls=%async_computation.15 | async-start | bytes 4718592 | tf_op jit(solution)/shard_map/reduce_scatter | solution.py:299
  422.5 406.1 %reduce-scatter.18.cloned.1.call-start = ((), (), s32[]{:S(2)}) async-start(), calls=%async_computation.16 | async-start | bytes 18874368 | tf_op jit(solution)/shard_map/reduce_scatter | solution.py:300
  435.3 513.3 %reduce-scatter.20.cloned.1.call-start = ((), (), s32[]{:S(2)}) async-start(), calls=%async_computation.17 | async-start | bytes 18874368 | tf_op jit(solution)/shard_map/reduce_scatter | solution.py:302
  447.6 108.0 %copy-start.12 = (bf16[128,2048]{1,0:T(8,128)(2,1)S(1)}, bf16[128,2048]{1,0:T(8,128)(2,1)}, u32[]{:S(2)}) copy-start(bf16[128,2048]{1,0:T(8,128)(2,1)} %param.26) | copy-start | bytes 1572868
  600.0 349.1 %copy-start.37 = (f32[64]{0:T(128)}, f32[64]{0:T(128)S(1)}, u32[]{:S(2)}) copy-start(f32[64]{0:T(128)S(1)} %dynamic-slice.2) | copy-start | bytes 772
  (35 other events, 551.8 us)
Sparse Core Ops, SparseCore 0:
  58.0 46.2 all-gather.7
  105.9 44.6 all-gather.15
  152.4 32.1 all-gather.9
  186.4 54.8 all-gather.11
  243.0 116.5 all-gather.13
  363.1 33.6 reduce-scatter.21
  399.1 76.7 reduce-scatter.11
  478.2 77.2 reduce-scatter.9
  559.4 93.4 reduce-scatter.13
  657.1 51.3 reduce-scatter.15
  712.6 115.9 reduce-scatter.17
  832.6 115.9 reduce-scatter.19
